TPU v7x, 32 devices: a whole 2x2x4 slice. The times are simulated.
32 devices in a mesh: depth: 8 (over y, x, core), rows: 4 (over z).
Axes of the slice: x: 2, y: 2, z: 4, core: 2. Of those that a mesh axis runs over, the one named last changes fastest.
Arguments:
- ref_feat: bfloat16 [2, 8, 5120], P(None, 'rows'), may hold values from -6 to 6
- src_feat: bfloat16 [2, 4, 8, 5120], P(None, None, 'rows'), may hold values from -6 to 6
- block_index: int32 [2, 4, 48, 4], P(None, None, 'depth', 'rows'), may hold values from 0 to 2, as said below
- blend: bfloat16 [2, 4, 48, 8, 160], P(None, None, 'depth', 'rows'), may hold values from 0 to 1
- conv_first: bfloat16 [3, 3, 3, 32, 40], replicated, may hold values from -0.1875 to 0.1875
- bias_first: float32 [32], replicated, may hold values from -3 to 3
- conv_second: bfloat16 [3, 3, 3, 32, 32], replicated, may hold values from -0.21875 to 0.21875
- bias_second: float32 [32], replicated, may hold values from -3 to 3
Outputs:
- regularized: bfloat16 [2, 48, 8, 5120], P(None, 'depth', 'rows')
Inputs may be any that keep to these rules, and one draw needn't show every extreme that they name: block_index[b, v, d, q] is q - 1 or q, held within 0 to 2, so rows of block q blend source row blocks block_index and block_index + 1.
All inputs are finite; a program needn't handle non-finite values.
Results may differ from a plain program's by a relative error of at most 0.0046.
Values may be sent and summed in bfloat16 or wider, within the bound.
A program may use at most 64 MiB of HBM per device.

v0:
```python
import jax
import jax.numpy as jnp
from jax import lax
from jax.sharding import PartitionSpec as P


def extended(block, sides, width):
    for axis, dim in sides:
        count = lax.axis_size(axis)
        forward = [(i, i + 1) for i in range(count - 1)]
        backward = [(target, source) for source, target in forward]
        low = lax.ppermute(
            lax.slice_in_dim(block, block.shape[dim] - width, None, axis=dim), axis, forward
        )
        high = lax.ppermute(lax.slice_in_dim(block, 0, width, axis=dim), axis, backward)
        block = jnp.concatenate([low, block, high], axis=dim)
    return block


def cost_plane(ref_rows, top_rows, bottom_rows, weight, feat_count, columns, groups):
    scenes = top_rows.shape[0]
    source_views = top_rows.shape[1]
    row_count = top_rows.shape[2]
    reference_cube = ref_rows.astype(jnp.float32).reshape(scenes, 1, row_count, feat_count, columns)
    blend_weight = weight.astype(jnp.float32)[:, :, :, None, :]
    upper_part = top_rows.astype(jnp.float32).reshape(
        scenes, source_views, row_count, feat_count, columns
    )
    lower_part = bottom_rows.astype(jnp.float32).reshape(
        scenes, source_views, row_count, feat_count, columns
    )
    warped = blend_weight * upper_part + (1.0 - blend_weight) * lower_part
    average = (reference_cube[:, 0] + jnp.sum(warped, axis=1)) / (source_views + 1.0)
    spread = (
        (reference_cube[:, 0] - average) ** 2 + jnp.sum((warped - average[:, None]) ** 2, axis=1)
    ) / (source_views + 1.0)
    per_group = feat_count // groups
    products = (reference_cube * warped).reshape(
        scenes, source_views, row_count, groups, per_group, columns
    )
    correlation = jnp.sum(products, axis=(1, 4)) / (source_views * per_group * 1.0)
    stacked = jnp.concatenate([correlation, spread], axis=2).astype(jnp.bfloat16)
    return stacked.reshape(scenes, row_count, (groups + feat_count) * columns)


def convolve(volume, kernel, shift_bias, out_planes, out_rows, columns):
    scenes = volume.shape[0]
    channels = kernel.shape[4]
    shaped = volume.reshape(scenes, volume.shape[1], volume.shape[2], channels, columns)
    padded = jnp.pad(shaped, ((0, 0), (0, 0), (0, 0), (0, 0), (1, 1)))
    summed = jnp.zeros((scenes, out_planes, out_rows, kernel.shape[3], columns), jnp.float32)
    for tap_depth in range(3):
        for tap_row in range(3):
            for tap_col in range(3):
                piece = padded[
                    :,
                    tap_depth : tap_depth + out_planes,
                    tap_row : tap_row + out_rows,
                    :,
                    tap_col : tap_col + columns,
                ]
                summed = summed + jnp.einsum(
                    "bprcw,oc->bprow",
                    piece,
                    kernel[tap_depth, tap_row, tap_col],
                    preferred_element_type=jnp.float32,
                )
    return summed + shift_bias[None, None, None, :, None]


def body(ref_feat, src_feat, block_index, blend, conv_first, bias_first, conv_second, bias_second):
    scenes = src_feat.shape[0]
    row_count = src_feat.shape[2]
    packed = src_feat.shape[3]
    planes = blend.shape[2]
    columns = blend.shape[4]
    channels = conv_first.shape[4]
    feat_count = packed // columns
    groups = channels - feat_count
    nearby = extended(src_feat, (("rows", 2),), row_count)
    lower_rim = nearby[:, :, :row_count]
    upper_rim = nearby[:, :, 2 * row_count :]
    offset = block_index[:, :, :, 0] - lax.axis_index("rows")

    def plane_cost(inputs):
        plane_offset, weight = inputs
        below = (plane_offset < 0)[:, :, None, None]
        top_rows = jnp.where(below, lower_rim, src_feat)
        bottom_rows = jnp.where(below, src_feat, upper_rim)
        return cost_plane(ref_feat, top_rows, bottom_rows, weight, feat_count, columns, groups)

    cost_planes = lax.map(plane_cost, (jnp.moveaxis(offset, 2, 0), jnp.moveaxis(blend, 2, 0)))
    volume = jnp.moveaxis(cost_planes, 0, 1)
    margin = extended(volume, (("depth", 1), ("rows", 2)), 1)
    hidden = jnp.maximum(convolve(margin, conv_first, bias_first, planes, row_count, columns), 0.0)
    hidden = hidden.astype(jnp.bfloat16).reshape(scenes, planes, row_count, -1)
    hidden_wide = extended(hidden, (("depth", 1), ("rows", 2)), 1)
    result = convolve(hidden_wide, conv_second, bias_second, planes, row_count, columns)
    return result.astype(jnp.bfloat16).reshape(scenes, planes, row_count, -1)


def solution(mesh):
    in_specs = (
        P(None, "rows", None),
        P(None, None, "rows", None),
        P(None, None, "depth", "rows"),
        P(None, None, "depth", "rows", None),
        P(),
        P(),
        P(),
        P(),
    )
    out_specs = P(None, "depth", "rows", None)
    return jax.shard_map(body, mesh=mesh, in_specs=in_specs, out_specs=out_specs, check_vma=False)
```

profile of v0, /device:TPU:0, one launch (start us, length us, event | category | flops | bytes accessed | tf_op | source)
XLA Modules:
  0.0 114.3 jit_solution(16075624221401118785)
XLA Ops:
  0.0 5.0 %collective-permute-start = (bf16[2,4,2,5120]{3,2,1,0:T(2,128)(2,1)}, bf16[2,4,2,5120]{3,2,1,0:T(2,128)(2,1)S(1)}, u32[]{:S(2)}, u32[]{:S(2)}) collective-permute-start(bf16[2,4,2,5120]{3,2,1,0:T(2,128)(2,1)} %param.11), channel_id=1, source_target_pairs={{0,1},{1,2},{2,3},{4,5},{5,6},{6,7},{8,9},{9,10},{10,11},{12,13},{... | collective-permute-start | bytes 491528 | tf_op jit(solution)/shard_map/ppermute | solution.py:12
  5.0 1.3 %collective-permute-start.1 = (bf16[2,4,2,5120]{3,2,1,0:T(2,128)(2,1)}, bf16[2,4,2,5120]{3,2,1,0:T(2,128)(2,1)S(1)}, u32[]{:S(2)}, u32[]{:S(2)}) collective-permute-start(bf16[2,4,2,5120]{3,2,1,0:T(2,128)(2,1)} %param.11), channel_id=1, source_target_pairs={{1,0},{2,1},{3,2},{5,4},{6,5},{7,6},{9,8},{10,9},{11,10},{13,12},{... | collective-permute-start | bytes 491528 | tf_op jit(solution)/shard_map/ppermute | solution.py:15
  6.3 0.8 copy.67
  7.1 0.7 broadcast_subtract_fusion.1
  7.9 0.8 collective-permute-done
  8.7 4.0 %collective-permute-done.1 = bf16[2,4,2,5120]{3,2,1,0:T(2,128)(2,1)S(1)} collective-permute-done((bf16[2,4,2,5120]{3,2,1,0:T(2,128)(2,1)}, bf16[2,4,2,5120]{3,2,1,0:T(2,128)(2,1)S(1)}, u32[]{:S(2)}, u32[]{:S(2)}) %collective-permute-start.1) | collective-permute-done | bytes 163872 | tf_op jit(solution)/shard_map/ppermute | solution.py:15
  12.7 29.4 %while.10 = (s32[]{:T(128)}, bf16[6,2,2,6400]{3,2,1,0:T(2,128)(2,1)S(1)}, bf16[2,2,5120]{2,1,0:T(2,128)(2,1)}, bf16[6,2,4,2,160]{4,3,2,1,0:T(2,128)(2,1)S(1)}, s...) while((s32[]{:T(128)}, ...), condition=%wide.region_4.5_spmd, body=%wide.region_0.4_spmd.sunk | while | flops 2490890 | bytes 6103269 | solution.py:92
  13.1 1.2 %reshape.219 = bf16[2,4,2,32,160]{4,3,2,1,0:T(8,128)(2,1)S(1)} reshape(bf16[2,4,2,5120]{3,2,1,0:T(2,128)(2,1)} %get-tuple-element.153) | data formatting | bytes 327680 | tf_op jit(solution)/shard_map/reshape.111
  16.8 0.6 multiply_reduce_fusion.5
  18.0 1.2 %reshape.219 = bf16[2,4,2,32,160]{4,3,2,1,0:T(8,128)(2,1)S(1)} reshape(bf16[2,4,2,5120]{3,2,1,0:T(2,128)(2,1)} %get-tuple-element.153) | data formatting | bytes 327680 | tf_op jit(solution)/shard_map/reshape.111
  21.7 0.6 multiply_reduce_fusion.5
  22.9 1.2 %reshape.219 = bf16[2,4,2,32,160]{4,3,2,1,0:T(8,128)(2,1)S(1)} reshape(bf16[2,4,2,5120]{3,2,1,0:T(2,128)(2,1)} %get-tuple-element.153) | data formatting | bytes 327680 | tf_op jit(solution)/shard_map/reshape.111
  26.6 0.6 multiply_reduce_fusion.5
  27.8 1.2 %reshape.219 = bf16[2,4,2,32,160]{4,3,2,1,0:T(8,128)(2,1)S(1)} reshape(bf16[2,4,2,5120]{3,2,1,0:T(2,128)(2,1)} %get-tuple-element.153) | data formatting | bytes 327680 | tf_op jit(solution)/shard_map/reshape.111
  31.5 0.6 multiply_reduce_fusion.5
  32.7 1.2 %reshape.219 = bf16[2,4,2,32,160]{4,3,2,1,0:T(8,128)(2,1)S(1)} reshape(bf16[2,4,2,5120]{3,2,1,0:T(2,128)(2,1)} %get-tuple-element.153) | data formatting | bytes 327680 | tf_op jit(solution)/shard_map/reshape.111
  36.4 0.6 multiply_reduce_fusion.5
  37.6 1.2 %reshape.219 = bf16[2,4,2,32,160]{4,3,2,1,0:T(8,128)(2,1)S(1)} reshape(bf16[2,4,2,5120]{3,2,1,0:T(2,128)(2,1)} %get-tuple-element.153) | data formatting | bytes 327680 | tf_op jit(solution)/shard_map/reshape.111
  41.3 0.6 multiply_reduce_fusion.5
  42.2 1.3 %collective-permute-start.2 = (bf16[2,1,2,6400]{3,2,0,1:T(2,128)(2,1)S(1)}, bf16[2,1,2,6400]{3,2,0,1:T(2,128)(2,1)S(1)}, u32[]{:S(2)}, u32[]{:S(2)}) collective-permute-start(bf16[2,1,2,6400]{3,2,0,1:T(2,128)(2,1)S(1)} %get-tuple-element.76), channel_id=1, source_target_pairs={{0,4},{4,8},{8,12},{12,16},{16,20},{20,24},{24,28},{1,5},{5,9},{9,... | collective-permute-start | bytes 153608 | tf_op jit(solution)/shard_map/ppermute | solution.py:12
  43.5 1.3 %collective-permute-start.3 = (bf16[2,1,2,6400]{3,2,0,1:T(2,128)(2,1)S(1)}, bf16[2,1,2,6400]{3,2,0,1:T(2,128)(2,1)S(1)}, u32[]{:S(2)}, u32[]{:S(2)}) collective-permute-start(bf16[2,1,2,6400]{3,2,0,1:T(2,128)(2,1)S(1)} %get-tuple-element.77), channel_id=1, source_target_pairs={{4,0},{8,4},{12,8},{16,12},{20,16},{24,20},{28,24},{5,1},{9,5},{13... | collective-permute-start | bytes 153608 | tf_op jit(solution)/shard_map/ppermute | solution.py:15
  44.9 3.5 %collective-permute-done.3 = bf16[2,1,2,6400]{3,2,0,1:T(2,128)(2,1)S(1)} collective-permute-done((bf16[2,1,2,6400]{3,2,0,1:T(2,128)(2,1)S(1)}, bf16[2,1,2,6400]{3,2,0,1:T(2,128)(2,1)S(1)}, u32[]{:S(2)}, u32[]{:S(2)}) %collective-permute-start.3) | collective-permute-done | bytes 51232 | tf_op jit(solution)/shard_map/ppermute | solution.py:15
  48.4 0.6 pad_maximum_fusion.3
  49.0 0.6 fusion.239
  49.6 3.5 %collective-permute-start.4 = (bf16[2,8,1,6400]{3,2,0,1:T(2,128)(2,1)S(1)}, bf16[2,8,1,6400]{3,2,0,1:T(2,128)(2,1)S(1)}, u32[]{:S(2)}, u32[]{:S(2)}) collective-permute-start(bf16[2,8,1,6400]{3,2,0,1:T(2,128)(2,1)S(1)} %get-tuple-element.72), channel_id=1, source_target_pairs={{0,1},{1,2},{2,3},{4,5},{5,6},{6,7},{8,9},{9,10},{10,11},{12,13},{... | collective-permute-start | bytes 614408 | tf_op jit(solution)/shard_map/ppermute | solution.py:12
  53.1 1.5 %collective-permute-start.5 = (bf16[2,8,1,6400]{3,2,0,1:T(2,128)(2,1)S(1)}, bf16[2,8,1,6400]{3,2,0,1:T(2,128)(2,1)S(1)}, u32[]{:S(2)}, u32[]{:S(2)}) collective-permute-start(bf16[2,8,1,6400]{3,2,0,1:T(2,128)(2,1)S(1)} %get-tuple-element.73), channel_id=1, source_target_pairs={{1,0},{2,1},{3,2},{5,4},{6,5},{7,6},{9,8},{10,9},{11,10},{13,12},{... | collective-permute-start | bytes 614408 | tf_op jit(solution)/shard_map/ppermute | solution.py:15
  54.6 6.5 %collective-permute-done.4 = bf16[2,8,1,6400]{3,2,0,1:T(2,128)(2,1)S(1)} collective-permute-done((bf16[2,8,1,6400]{3,2,0,1:T(2,128)(2,1)S(1)}, bf16[2,8,1,6400]{3,2,0,1:T(2,128)(2,1)S(1)}, u32[]{:S(2)}, u32[]{:S(2)}) %collective-permute-start.4) | collective-permute-done | bytes 204832 | tf_op jit(solution)/shard_map/ppermute | solution.py:12
  61.1 4.7 %collective-permute-done.5 = bf16[2,8,1,6400]{3,2,0,1:T(2,128)(2,1)S(1)} collective-permute-done((bf16[2,8,1,6400]{3,2,0,1:T(2,128)(2,1)S(1)}, bf16[2,8,1,6400]{3,2,0,1:T(2,128)(2,1)S(1)}, u32[]{:S(2)}, u32[]{:S(2)}) %collective-permute-start.5) | collective-permute-done | bytes 204832 | tf_op jit(solution)/shard_map/ppermute | solution.py:15
  65.8 1.4 %pad_maximum_fusion.1 = bf16[2,8,4,6400]{3,2,0,1:T(4,128)(2,1)S(1)} fusion(bf16[2,8,1,6400]{3,2,0,1:T(2,128)(2,1)S(1)} %collective-permute-done.5, bf16[2,1,2,6400]{3,2,0,1:T(2,128)(2,1)S(1)} %collective-permute-done.3, bf16[2,6,2,6400]{3,2,0,1:T(2,128)(2,1)S(1)} %bitcast.511, bf16[2,1,2,6400]{3,2,0,1:T(2,128)(2,1)S(1)} %collective-permute-done.2, ...), kind=kLoop, calls=%fused_computation.93 | loop fusion | flops 4096000 | bytes 1638400 | tf_op jit(solution)/shard_map/concatenate | solution.py:16
  67.5 1.8 %reshape.151 = bf16[2,8,4,40,160]{4,3,2,1,0:T(8,128)(2,1)S(1)} reshape(bf16[2,8,4,6400]{3,2,1,0:T(4,128)(2,1)S(1)} %copy.11) | data formatting | bytes 1638400 | tf_op jit(solution)/shard_map/reshape | solution.py:49
  69.3 0.3 fusion.61
  69.6 0.3 fusion.63
  70.0 0.3 fusion.65
  70.3 0.3 fusion.57
  70.7 0.3 fusion.59
  71.0 0.3 fusion.53
  71.4 0.3 fusion.55
  71.7 0.3 fusion.49
  72.1 0.3 fusion.51
  72.4 0.3 fusion.45
  72.8 0.3 fusion.47
  73.1 0.3 convolution_bitcast_fusion.18
  73.5 0.3 convolution_bitcast_fusion.19
  73.8 0.3 convolution_bitcast_fusion.16
  74.2 0.3 convolution_bitcast_fusion.17
  74.5 0.3 convolution_bitcast_fusion.14
  74.9 0.3 convolution_bitcast_fusion.15
  75.2 0.3 convolution_bitcast_fusion.13
  77.9 0.4 copy-done.4
  78.5 0.6 reshape.152
  79.2 3.3 %collective-permute-start.6 = (bf16[2,1,2,5120]{3,2,1,0:T(2,128)(2,1)S(1)}, bf16[2,1,2,5120]{3,2,1,0:T(2,128)(2,1)S(1)}, u32[]{:S(2)}, u32[]{:S(2)}) collective-permute-start(bf16[2,1,2,5120]{3,2,1,0:T(2,128)(2,1)S(1)} %get-tuple-element.79), channel_id=1, source_target_pairs={{0,4},{4,8},{8,12},{12,16},{16,20},{20,24},{24,28},{1,5},{5,9},{9,... | collective-permute-start | bytes 122888 | tf_op jit(solution)/shard_map/ppermute | solution.py:12
  82.5 1.5 %collective-permute-start.7 = (bf16[2,1,2,5120]{3,2,1,0:T(2,128)(2,1)S(1)}, bf16[2,1,2,5120]{3,2,1,0:T(2,128)(2,1)S(1)}, u32[]{:S(2)}, u32[]{:S(2)}) collective-permute-start(bf16[2,1,2,5120]{3,2,1,0:T(2,128)(2,1)S(1)} %get-tuple-element.78), channel_id=1, source_target_pairs={{4,0},{8,4},{12,8},{16,12},{20,16},{24,20},{28,24},{5,1},{9,5},{13... | collective-permute-start | bytes 122888 | tf_op jit(solution)/shard_map/ppermute | solution.py:15
  84.3 2.5 %collective-permute-done.7 = bf16[2,1,2,5120]{3,2,1,0:T(2,128)(2,1)S(1)} collective-permute-done((bf16[2,1,2,5120]{3,2,1,0:T(2,128)(2,1)S(1)}, bf16[2,1,2,5120]{3,2,1,0:T(2,128)(2,1)S(1)}, u32[]{:S(2)}, u32[]{:S(2)}) %collective-permute-start.7) | collective-permute-done | bytes 40992 | tf_op jit(solution)/shard_map/ppermute | solution.py:15
  86.8 0.5 fusion.240
  87.3 3.5 %collective-permute-start.8 = (bf16[2,8,1,5120]{3,2,1,0:T(2,128)(2,1)S(1)}, bf16[2,8,1,5120]{3,2,1,0:T(2,128)(2,1)S(1)}, u32[]{:S(2)}, u32[]{:S(2)}) collective-permute-start(bf16[2,8,1,5120]{3,2,1,0:T(2,128)(2,1)S(1)} %get-tuple-element.74), channel_id=1, source_target_pairs={{0,1},{1,2},{2,3},{4,5},{5,6},{6,7},{8,9},{9,10},{10,11},{12,13},{... | collective-permute-start | bytes 491528 | tf_op jit(solution)/shard_map/ppermute | solution.py:12
  90.8 1.4 %collective-permute-start.9 = (bf16[2,8,1,5120]{3,2,1,0:T(2,128)(2,1)S(1)}, bf16[2,8,1,5120]{3,2,1,0:T(2,128)(2,1)S(1)}, u32[]{:S(2)}, u32[]{:S(2)}) collective-permute-start(bf16[2,8,1,5120]{3,2,1,0:T(2,128)(2,1)S(1)} %get-tuple-element.75), channel_id=1, source_target_pairs={{1,0},{2,1},{3,2},{5,4},{6,5},{7,6},{9,8},{10,9},{11,10},{13,12},{... | collective-permute-start | bytes 491528 | tf_op jit(solution)/shard_map/ppermute | solution.py:15
  92.2 4.9 %collective-permute-done.8 = bf16[2,8,1,5120]{3,2,1,0:T(2,128)(2,1)S(1)} collective-permute-done((bf16[2,8,1,5120]{3,2,1,0:T(2,128)(2,1)S(1)}, bf16[2,8,1,5120]{3,2,1,0:T(2,128)(2,1)S(1)}, u32[]{:S(2)}, u32[]{:S(2)}) %collective-permute-start.8) | collective-permute-done | bytes 163872 | tf_op jit(solution)/shard_map/ppermute | solution.py:12
  97.1 4.8 %collective-permute-done.9 = bf16[2,8,1,5120]{3,2,1,0:T(2,128)(2,1)S(1)} collective-permute-done((bf16[2,8,1,5120]{3,2,1,0:T(2,128)(2,1)S(1)}, bf16[2,8,1,5120]{3,2,1,0:T(2,128)(2,1)S(1)}, u32[]{:S(2)}, u32[]{:S(2)}) %collective-permute-start.9) | collective-permute-done | bytes 163872 | tf_op jit(solution)/shard_map/ppermute | solution.py:15
  102.0 1.1 pad_maximum_fusion.2
  103.1 1.3 %reshape.153 = bf16[2,8,4,32,160]{4,3,2,1,0:T(8,128)(2,1)S(1)} reshape(bf16[2,8,4,5120]{3,2,1,0:T(4,128)(2,1)S(1)} %pad_maximum_fusion.2) | data formatting | bytes 1310720 | tf_op jit(solution)/shard_map/reshape | solution.py:49
  106.8 0.3 convolution_add_fusion.14
  108.6 0.3 convolution_add_fusion.8
  112.3 0.4 copy-done.5
  113.0 1.3 %reshape.154 = bf16[2,6,2,5120]{3,2,1,0:T(2,128)(2,1)} reshape(bf16[2,6,2,32,160]{4,3,2,1,0:T(8,128)(2,1)S(1)} %fusion.36) | data formatting | bytes 491520 | tf_op jit(solution)/shard_map/reshape | solution.py:99
  (194 shorter events, 28.1 us)
Async XLA Ops:
  0.0 8.7 %collective-permute-start = (bf16[2,4,2,5120]{3,2,1,0:T(2,128)(2,1)}, bf16[2,4,2,5120]{3,2,1,0:T(2,128)(2,1)S(1)}, u32[]{:S(2)}, u32[]{:S(2)}) collective-permute-start(bf16[2,4,2,5120]{3,2,1,0:T(2,128)(2,1)} %param.11), channel_id=1, source_target_pairs={{0,1},{1,2},{2,3},{4,5},{5,6},{6,7},{8,9},{9,10},{10,11},{12,13},{... | collective-permute-start | bytes 491528 | tf_op jit(solution)/shard_map/ppermute | solution.py:12
  5.0 7.8 %collective-permute-start.1 = (bf16[2,4,2,5120]{3,2,1,0:T(2,128)(2,1)}, bf16[2,4,2,5120]{3,2,1,0:T(2,128)(2,1)S(1)}, u32[]{:S(2)}, u32[]{:S(2)}) collective-permute-start(bf16[2,4,2,5120]{3,2,1,0:T(2,128)(2,1)} %param.11), channel_id=1, source_target_pairs={{1,0},{2,1},{3,2},{5,4},{6,5},{7,6},{9,8},{10,9},{11,10},{13,12},{... | collective-permute-start | bytes 491528 | tf_op jit(solution)/shard_map/ppermute | solution.py:15
  12.7 2.4 %copy-start.1 = (bf16[2,2,5120]{2,1,0:T(2,128)(2,1)S(1)}, bf16[2,2,5120]{2,1,0:T(2,128)(2,1)}, u32[]{:S(2)}) copy-start(bf16[2,2,5120]{2,1,0:T(2,128)(2,1)} %get-tuple-element.149) | copy-start | bytes 122884 | tf_op jit(solution)/shard_map/while
  14.9 1.0 copy-start
  17.6 2.4 %copy-start.1 = (bf16[2,2,5120]{2,1,0:T(2,128)(2,1)S(1)}, bf16[2,2,5120]{2,1,0:T(2,128)(2,1)}, u32[]{:S(2)}) copy-start(bf16[2,2,5120]{2,1,0:T(2,128)(2,1)} %get-tuple-element.149) | copy-start | bytes 122884 | tf_op jit(solution)/shard_map/while
  19.8 1.0 copy-start
  22.5 2.4 %copy-start.1 = (bf16[2,2,5120]{2,1,0:T(2,128)(2,1)S(1)}, bf16[2,2,5120]{2,1,0:T(2,128)(2,1)}, u32[]{:S(2)}) copy-start(bf16[2,2,5120]{2,1,0:T(2,128)(2,1)} %get-tuple-element.149) | copy-start | bytes 122884 | tf_op jit(solution)/shard_map/while
  24.7 1.0 copy-start
  27.4 2.4 %copy-start.1 = (bf16[2,2,5120]{2,1,0:T(2,128)(2,1)S(1)}, bf16[2,2,5120]{2,1,0:T(2,128)(2,1)}, u32[]{:S(2)}) copy-start(bf16[2,2,5120]{2,1,0:T(2,128)(2,1)} %get-tuple-element.149) | copy-start | bytes 122884 | tf_op jit(solution)/shard_map/while
  29.7 1.0 copy-start
  32.4 2.4 %copy-start.1 = (bf16[2,2,5120]{2,1,0:T(2,128)(2,1)S(1)}, bf16[2,2,5120]{2,1,0:T(2,128)(2,1)}, u32[]{:S(2)}) copy-start(bf16[2,2,5120]{2,1,0:T(2,128)(2,1)} %get-tuple-element.149) | copy-start | bytes 122884 | tf_op jit(solution)/shard_map/while
  34.6 1.0 copy-start
  37.3 2.4 %copy-start.1 = (bf16[2,2,5120]{2,1,0:T(2,128)(2,1)S(1)}, bf16[2,2,5120]{2,1,0:T(2,128)(2,1)}, u32[]{:S(2)}) copy-start(bf16[2,2,5120]{2,1,0:T(2,128)(2,1)} %get-tuple-element.149) | copy-start | bytes 122884 | tf_op jit(solution)/shard_map/while
  39.5 1.0 copy-start
  42.2 2.6 %collective-permute-start.2 = (bf16[2,1,2,6400]{3,2,0,1:T(2,128)(2,1)S(1)}, bf16[2,1,2,6400]{3,2,0,1:T(2,128)(2,1)S(1)}, u32[]{:S(2)}, u32[]{:S(2)}) collective-permute-start(bf16[2,1,2,6400]{3,2,0,1:T(2,128)(2,1)S(1)} %get-tuple-element.76), channel_id=1, source_target_pairs={{0,4},{4,8},{8,12},{12,16},{16,20},{20,24},{24,28},{1,5},{5,9},{9,... | collective-permute-start | bytes 153608 | tf_op jit(solution)/shard_map/ppermute | solution.py:12
  43.5 4.9 %collective-permute-start.3 = (bf16[2,1,2,6400]{3,2,0,1:T(2,128)(2,1)S(1)}, bf16[2,1,2,6400]{3,2,0,1:T(2,128)(2,1)S(1)}, u32[]{:S(2)}, u32[]{:S(2)}) collective-permute-start(bf16[2,1,2,6400]{3,2,0,1:T(2,128)(2,1)S(1)} %get-tuple-element.77), channel_id=1, source_target_pairs={{4,0},{8,4},{12,8},{16,12},{20,16},{24,20},{28,24},{5,1},{9,5},{13... | collective-permute-start | bytes 153608 | tf_op jit(solution)/shard_map/ppermute | solution.py:15
  49.6 11.5 %collective-permute-start.4 = (bf16[2,8,1,6400]{3,2,0,1:T(2,128)(2,1)S(1)}, bf16[2,8,1,6400]{3,2,0,1:T(2,128)(2,1)S(1)}, u32[]{:S(2)}, u32[]{:S(2)}) collective-permute-start(bf16[2,8,1,6400]{3,2,0,1:T(2,128)(2,1)S(1)} %get-tuple-element.72), channel_id=1, source_target_pairs={{0,1},{1,2},{2,3},{4,5},{5,6},{6,7},{8,9},{9,10},{10,11},{12,13},{... | collective-permute-start | bytes 614408 | tf_op jit(solution)/shard_map/ppermute | solution.py:12
  53.1 12.7 %collective-permute-start.5 = (bf16[2,8,1,6400]{3,2,0,1:T(2,128)(2,1)S(1)}, bf16[2,8,1,6400]{3,2,0,1:T(2,128)(2,1)S(1)}, u32[]{:S(2)}, u32[]{:S(2)}) collective-permute-start(bf16[2,8,1,6400]{3,2,0,1:T(2,128)(2,1)S(1)} %get-tuple-element.73), channel_id=1, source_target_pairs={{1,0},{2,1},{3,2},{5,4},{6,5},{7,6},{9,8},{10,9},{11,10},{13,12},{... | collective-permute-start | bytes 614408 | tf_op jit(solution)/shard_map/ppermute | solution.py:15
  67.5 1.8 %copy-start.2 = (bf16[3,3,3,32,40]{4,3,2,1,0:T(8,128)(2,1)S(1)}, bf16[3,3,3,32,40]{4,3,2,1,0:T(8,128)(2,1)}, u32[]{:S(2)}) copy-start(bf16[3,3,3,32,40]{4,3,2,1,0:T(8,128)(2,1)} %param.14) | copy-start | bytes 207364
  77.6 0.7 copy-start.4
  79.2 4.8 %collective-permute-start.6 = (bf16[2,1,2,5120]{3,2,1,0:T(2,128)(2,1)S(1)}, bf16[2,1,2,5120]{3,2,1,0:T(2,128)(2,1)S(1)}, u32[]{:S(2)}, u32[]{:S(2)}) collective-permute-start(bf16[2,1,2,5120]{3,2,1,0:T(2,128)(2,1)S(1)} %get-tuple-element.79), channel_id=1, source_target_pairs={{0,4},{4,8},{8,12},{12,16},{16,20},{20,24},{24,28},{1,5},{5,9},{9,... | collective-permute-start | bytes 122888 | tf_op jit(solution)/shard_map/ppermute | solution.py:12
  82.5 4.3 %collective-permute-start.7 = (bf16[2,1,2,5120]{3,2,1,0:T(2,128)(2,1)S(1)}, bf16[2,1,2,5120]{3,2,1,0:T(2,128)(2,1)S(1)}, u32[]{:S(2)}, u32[]{:S(2)}) collective-permute-start(bf16[2,1,2,5120]{3,2,1,0:T(2,128)(2,1)S(1)} %get-tuple-element.78), channel_id=1, source_target_pairs={{4,0},{8,4},{12,8},{16,12},{20,16},{24,20},{28,24},{5,1},{9,5},{13... | collective-permute-start | bytes 122888 | tf_op jit(solution)/shard_map/ppermute | solution.py:15
  87.3 9.8 %collective-permute-start.8 = (bf16[2,8,1,5120]{3,2,1,0:T(2,128)(2,1)S(1)}, bf16[2,8,1,5120]{3,2,1,0:T(2,128)(2,1)S(1)}, u32[]{:S(2)}, u32[]{:S(2)}) collective-permute-start(bf16[2,8,1,5120]{3,2,1,0:T(2,128)(2,1)S(1)} %get-tuple-element.74), channel_id=1, source_target_pairs={{0,1},{1,2},{2,3},{4,5},{5,6},{6,7},{8,9},{9,10},{10,11},{12,13},{... | collective-permute-start | bytes 491528 | tf_op jit(solution)/shard_map/ppermute | solution.py:12
  90.8 13.6 %copy-start.3 = (bf16[3,3,3,32,32]{4,3,2,1,0:T(8,128)(2,1)S(1)}, bf16[3,3,3,32,32]{4,3,2,1,0:T(8,128)(2,1)}, u32[]{:S(2)}) copy-start(bf16[3,3,3,32,32]{4,3,2,1,0:T(8,128)(2,1)} %param.16) | copy-start | bytes 165892
  90.8 11.2 %collective-permute-start.9 = (bf16[2,8,1,5120]{3,2,1,0:T(2,128)(2,1)S(1)}, bf16[2,8,1,5120]{3,2,1,0:T(2,128)(2,1)S(1)}, u32[]{:S(2)}, u32[]{:S(2)}) collective-permute-start(bf16[2,8,1,5120]{3,2,1,0:T(2,128)(2,1)S(1)} %get-tuple-element.75), channel_id=1, source_target_pairs={{1,0},{2,1},{3,2},{5,4},{6,5},{7,6},{9,8},{10,9},{11,10},{13,12},{... | collective-permute-start | bytes 491528 | tf_op jit(solution)/shard_map/ppermute | solution.py:15
  112.0 0.7 copy-start.5
where the time goes:
time: 117 us; the launch traced here: 114 us
  waiting for transfers between devices  31.8 us (27%)
  local copies, waits for them, and re-layouts  28.5 us (24%)
  starting transfers between devices  23.5 us (20%)
  matrix products  16.8 us (14%)
  other arithmetic  12 us (10%)
    ppermute x5, waiting for transfers between devices, extended(): lax.ppermute(lax.slice_in_dim(block, 0, width, axis=dim), axis, backward)  19.6 us
    dot_general x54, matrix products, convolve(): jnp.einsum('bprcw,oc->bprow', piece, kernel[tap_depth, tap_row, tap_col],...  16.8 us
    ppermute x5, starting transfers between devices, extended(): lax.ppermute(lax.slice_in_dim(block, block.shape[dim] - width, None, axis...  16.5 us
    another operation x36, local copies, waits for them, and re-layouts  15.6 us
    ppermute x5, waiting for transfers between devices, extended(): lax.ppermute(lax.slice_in_dim(block, block.shape[dim] - width, None, axis...  12.2 us
    ppermute x5, starting transfers between devices, extended(): lax.ppermute(lax.slice_in_dim(block, 0, width, axis=dim), axis, backward)  6.99 us
    reduce_sum x6, other arithmetic, cost_plane(): jnp.sum(products, axis=(1, 4)) / (source_views * per_group * 1.0)  3.56 us
    concatenate x3, other arithmetic, extended(): block = jnp.concatenate([low, block, high], axis=dim)  3.1 us
  transfers between devices with their start and end apart: 10, of which 8 were waited for; matrix products, arithmetic and copies ran while one was open for 2% of the time, Pallas kernels for 0%

commit v1 on v0

v1 whole, which is shorter than its diff:
```python
import functools

import jax
import jax.numpy as jnp
from jax import lax
from jax.experimental import pallas as pl
from jax.experimental.pallas import tpu as pltpu
from jax.sharding import PartitionSpec as P

MESH = pl.DeviceIdType.MESH
LANES = 128
NEAR = ((0, 1), (0, -1), (1, 0), (-1, 0), (1, 1), (1, -1), (-1, 1), (-1, -1))
FAR = ((0, 2), (0, -2))


def kernel(
    dims, feat_in, coef_in, k1_in, b1_in, k2_in, b2_in, out_ref,
    feat, coef, vol, hid, work, w1, w2, prep, bias, send_sem, recv_sem, local_sem,
):
    scenes, views, rows, planes, feats, groups, columns, regs, depth_n, rows_n = dims
    channels = groups + feats
    per_group = feats // groups
    packed = feat_in.shape[3]
    wide = 2 * LANES
    tail = columns - LANES
    d = lax.axis_index("depth")
    q = lax.axis_index("rows")

    def exists(dd, dq):
        return (d + dd >= 0) & (d + dd < depth_n) & (q + dq >= 0) & (q + dq < rows_n)

    barrier = pltpu.get_barrier_semaphore()
    for dd, dq in NEAR + FAR:
        @pl.when(exists(dd, dq))
        def _():
            pl.semaphore_signal(barrier, inc=1, device_id=(d + dd, q + dq), device_id_type=MESH)

    local = [
        pltpu.make_async_copy(feat_in, feat.at[2], local_sem.at[0]),
        pltpu.make_async_copy(coef_in, coef.at[1, pl.ds(2, planes)], local_sem.at[1]),
    ]
    for copy in local:
        copy.start()

    def feat_copy(dq, k):
        slot = 2 - dq
        count = views + 1 if abs(dq) == 1 else views
        return pltpu.make_async_remote_copy(
            src_ref=feat_in.at[pl.ds(0, count)],
            dst_ref=feat.at[slot, pl.ds(0, count)],
            send_sem=send_sem.at[k], recv_sem=recv_sem.at[k],
            device_id=(d, q + dq), device_id_type=MESH,
        )

    def coef_copy(dd, dq, k):
        if dd == 0:
            first, count, at = 0, planes, 2
        elif dd == 1:
            first, count, at = planes - 2, 2, 0
        else:
            first, count, at = 0, 2, planes + 2
        return pltpu.make_async_remote_copy(
            src_ref=coef_in.at[pl.ds(first, count)],
            dst_ref=coef.at[1 - dq, pl.ds(at, count)],
            send_sem=send_sem.at[k], recv_sem=recv_sem.at[k],
            device_id=(d + dd, q + dq), device_id_type=MESH,
        )

    near_feat = [((0, dq), feat_copy(dq, i)) for i, dq in enumerate((1, -1))]
    far_feat = [((0, dq), feat_copy(dq, 2 + i)) for i, dq in enumerate((2, -2))]
    depth_coef = [((dd, 0), coef_copy(dd, 0, 4 + i)) for i, dd in enumerate((1, -1))]
    side_coef = [
        ((dd, dq), coef_copy(dd, dq, 6 + i))
        for i, (dd, dq) in enumerate([m for m in NEAR if m[1] != 0])
    ]
    every = depth_coef + near_feat + side_coef + far_feat

    for slot, gone in ((0, q < 2), (1, q < 1), (3, q + 1 >= rows_n), (4, q + 2 >= rows_n)):
        @pl.when(gone)
        def _():
            feat[slot] = jnp.zeros(feat.shape[1:], feat.dtype)

    beside = 1 + lax.div(d + depth_n - 1, depth_n) + lax.div(2 * depth_n - 2 - d, depth_n)
    above = 1 + lax.div(q + rows_n - 1, rows_n) + lax.div(2 * rows_n - 2 - q, rows_n)
    beyond = lax.div(q + rows_n - 2, rows_n) + lax.div(2 * rows_n - 3 - q, rows_n)
    pl.semaphore_wait(barrier, beside * above - 1 + beyond)

    for (dd, dq), copy in every:
        @pl.when(exists(dd, dq))
        def _():
            copy.start()

    def arrive(pairs):
        for (dd, dq), copy in pairs:
            @pl.when(exists(-dd, -dq))
            def _():
                copy.wait_recv()

    def place(kernel_in, count, span, target, dest):
        for a in range(3):
            for r in range(3):
                line = jnp.zeros((regs, span), jnp.float32)
                for s in range(3):
                    c = lax.broadcasted_iota(jnp.int32, (count, span), 0)
                    k = lax.broadcasted_iota(jnp.int32, (count, span), 1)
                    pick = jnp.where(dest(s, c) == k, 1.0, 0.0).astype(jnp.bfloat16)
                    line = line + jnp.dot(kernel_in[a, r, s], pick, preferred_element_type=jnp.float32)
                line = line.astype(jnp.bfloat16)
                for j in range(rows):
                    target[pl.ds((a * rows + j) * regs, regs), pl.ds((j + r) * span, span)] = line

    def first_dest(s, c):
        f = c - groups
        spread_at = s * feats + (f % per_group) * groups + f // per_group
        return jnp.where(c < groups, 3 * feats + s * groups + c, spread_at)

    w1[...] = jnp.zeros(w1.shape, w1.dtype)
    w2[...] = jnp.zeros(w2.shape, w2.dtype)
    place(k1_in, channels, LANES, w1, first_dest)
    place(k2_in, regs, LANES, w2, lambda s, c: s * regs + c)
    eye = lax.broadcasted_iota(jnp.int32, (regs, regs), 0) == lax.broadcasted_iota(
        jnp.int32, (regs, regs), 1
    )
    for i, b_in in enumerate((b1_in, b2_in)):
        column = jnp.sum(jnp.where(eye, b_in[...], 0.0), axis=1, keepdims=True)
        bias[i] = jnp.broadcast_to(jnp.concatenate([column] * rows, axis=0), (rows * regs, wide))

    for copy in local:
        copy.wait()

    lane = lax.broadcasted_iota(jnp.int32, (groups, LANES), 1)
    in_tail = lane < tail

    def unpack(tail_packed):
        parts = []
        for j in range(per_group):
            part = tail_packed if j == 0 else pltpu.roll(tail_packed, LANES - tail * j, 1)
            parts.append(jnp.where(in_tail, part, 0.0))
        return parts

    def volume_rows(block):
        for b in range(scenes):
            for m in range(rows):
                ref = feat[block + 1, views, b, m].astype(jnp.float32)
                prep[3 * views] = ref
                for v in range(views):
                    low = feat[block, v, b, m].astype(jnp.float32)
                    mid = feat[block + 1, v, b, m].astype(jnp.float32)
                    up = feat[block + 2, v, b, m].astype(jnp.float32)
                    prep[v] = mid - ref
                    prep[views + v] = low - mid
                    prep[2 * views + v] = up - mid
                row = (block - 1) * rows + m
                row_ok = (q * rows + row >= 0) & (q * rows + row < rows_n * rows)

                def plane(p, carry):
                    at = d * planes + p - 2
                    ok = row_ok & (at >= 0) & (at < depth_n * planes)
                    weights = coef[block, p, b, m].astype(jnp.float32)
                    others = 1.0 - weights
                    total = None
                    for v in range(views):
                        cl = weights[v : v + 1]
                        cu = others[views + v : views + v + 1]
                        both = []
                        for lo, hi, l0 in ((0, feats, 0), (feats, packed, LANES)):
                            both.append(
                                prep[v, lo:hi]
                                + cl[:, l0 : l0 + LANES] * prep[views + v, lo:hi]
                                + cu[:, l0 : l0 + LANES] * prep[2 * views + v, lo:hi]
                            )
                        if total is None:
                            total = both
                            square = [u * u for u in both]
                        else:
                            total = [t + u for t, u in zip(total, both)]
                            square = [t + u * u for t, u in zip(square, both)]
                    share = 1.0 / (views + 1.0)
                    spread = [(s2 - t * t * share) * share for s2, t in zip(square, total)]
                    refs = [prep[3 * views, 0:feats], prep[3 * views, feats:packed]]
                    product = [r * (t + (1.0 * views) * r) for r, t in zip(refs, total)]
                    scale = 1.0 / (views * per_group)
                    head = product[0][0:groups]
                    for j in range(1, per_group):
                        head = head + product[0][j * groups : (j + 1) * groups]
                    rest = product[1]
                    step = LANES // 2
                    while step >= tail:
                        rest = rest + pltpu.roll(rest, step, 1)
                        step //= 2
                    corr = jnp.concatenate([head, jnp.where(in_tail, rest, 0.0)], axis=1) * scale
                    ends = unpack(spread[1])
                    full = jnp.concatenate(
                        [jnp.concatenate([spread[0], jnp.concatenate(ends, axis=0)], axis=1), corr],
                        axis=0,
                    )
                    full = jnp.where(ok, full, 0.0)
                    left = pltpu.roll(full, 1, 1)
                    right = pltpu.roll(full, wide - 1, 1)
                    lines = [left[:feats], full[:feats], right[:feats]]
                    lines += [left[feats:], full[feats:], right[feats:]]
                    lines.append(jnp.zeros((LANES - 3 * channels, wide), jnp.float32))
                    vol[b, p, row + rows] = jnp.concatenate(lines, axis=0).astype(jnp.bfloat16)
                    return carry

                lax.fori_loop(0, planes + 4, plane, 0)

    arrive(depth_coef)
    arrive(near_feat)
    volume_rows(1)
    arrive(side_coef)
    arrive(far_feat)
    volume_rows(0)
    volume_rows(2)

    size = rows * regs
    inside = lax.broadcasted_iota(jnp.int32, (regs, wide), 1) < columns
    for b in range(scenes):
        for pair in range(2):
            base = pair * rows

            def first(p, carry):
                piece = vol[b, p, pl.ds(base, rows + 2)].reshape((rows + 2) * LANES, wide)
                work[p] = jnp.dot(w1[...], piece, preferred_element_type=jnp.float32)
                return carry

            lax.fori_loop(0, planes + 4, first, 0)

            def hidden(p, carry):
                summed = (
                    work[p, 0:size] + work[p + 1, size : 2 * size]
                    + work[p + 2, 2 * size : 3 * size] + bias[0]
                )
                summed = jnp.maximum(summed, 0.0)
                at = d * planes + p - 1
                for j in range(rows):
                    row = q * rows + base + j - 1
                    ok = (at >= 0) & (at < depth_n * planes) & (row >= 0) & (row < rows_n * rows)
                    part = summed[j * regs : (j + 1) * regs]
                    part = jnp.where(inside & ok, part, 0.0)
                    part = part.astype(jnp.bfloat16).astype(jnp.float32)
                    lines = [pltpu.roll(part, 1, 1), part, pltpu.roll(part, wide - 1, 1)]
                    lines.append(jnp.zeros((LANES - 3 * regs, wide), jnp.float32))
                    hid[b, p, base + j] = jnp.concatenate(lines, axis=0).astype(jnp.bfloat16)
                return carry

            lax.fori_loop(0, planes + 2, hidden, 0)

        def second(p, carry):
            piece = hid[b, p].reshape((rows + 2) * LANES, wide)
            work[p] = jnp.dot(w2[...], piece, preferred_element_type=jnp.float32)
            return carry

        lax.fori_loop(0, planes + 2, second, 0)

        def finish(p, carry):
            summed = (
                work[p, 0:size] + work[p + 1, size : 2 * size]
                + work[p + 2, 2 * size : 3 * size] + bias[1]
            )
            for j in range(rows):
                out_ref[b, p, j] = summed[j * regs : (j + 1) * regs, 0:columns].astype(jnp.bfloat16)
            return carry

        lax.fori_loop(0, planes, finish, 0)

    for (dd, dq), copy in every:
        @pl.when(exists(dd, dq))
        def _():
            copy.wait_send()


def body(
    depth_n, rows_n, ref_feat, src_feat, block_index, blend, conv_first, bias_first, conv_second, bias_second
):
    scenes, views, rows, flat = src_feat.shape
    planes, columns = blend.shape[2], blend.shape[4]
    channels, regs = conv_first.shape[4], conv_first.shape[3]
    feats = flat // columns
    groups = channels - feats
    per_group = feats // groups
    tail = columns - LANES
    packed = feats + groups

    cube = jnp.concatenate([src_feat, ref_feat[:, None]], axis=1)
    cube = cube.reshape(scenes, views + 1, rows, groups, per_group, columns)
    main = jnp.moveaxis(cube[..., :LANES], 4, 3).reshape(scenes, views + 1, rows, feats, LANES)
    ends = cube[..., LANES:].reshape(scenes, views + 1, rows, groups, per_group * tail)
    feat_in = jnp.moveaxis(jnp.concatenate([main, ends], axis=3), 1, 0)

    below = (block_index < lax.axis_index("rows"))[:, :, :, :, None]
    lower = jnp.where(below, blend, jnp.zeros_like(blend))
    upper = jnp.where(below, jnp.ones_like(blend), blend)
    coef = jnp.concatenate([lower, upper], axis=1)
    coef = jnp.concatenate([coef[..., :LANES]] + [coef[..., LANES:]] * per_group, axis=4)
    coef_in = jnp.transpose(coef, (2, 0, 3, 1, 4))

    wide = 2 * LANES
    dims = (scenes, views, rows, planes, feats, groups, columns, regs, depth_n, rows_n)
    bf16, f32 = jnp.bfloat16, jnp.float32
    out = pl.pallas_call(
        functools.partial(kernel, dims),
        out_shape=jax.ShapeDtypeStruct((scenes, planes, rows, regs, columns), bf16),
        in_specs=[pl.BlockSpec(memory_space=pltpu.VMEM)] * 6,
        out_specs=pl.BlockSpec(memory_space=pltpu.VMEM),
        scratch_shapes=[
            pltpu.VMEM((5, views + 1, scenes, rows, packed, LANES), bf16),
            pltpu.VMEM((3, planes + 4, scenes, rows, 2 * views, wide), bf16),
            pltpu.VMEM((scenes, planes + 4, 3 * rows, LANES, wide), bf16),
            pltpu.VMEM((scenes, planes + 2, rows + 2, LANES, wide), bf16),
            pltpu.VMEM((planes + 4, 3 * rows * regs, wide), f32),
            pltpu.VMEM((3 * rows * regs, (rows + 2) * LANES), bf16),
            pltpu.VMEM((3 * rows * regs, (rows + 2) * LANES), bf16),
            pltpu.VMEM((3 * views + 1, packed, LANES), f32),
            pltpu.VMEM((2, rows * regs, wide), f32),
            pltpu.SemaphoreType.DMA((12,)),
            pltpu.SemaphoreType.DMA((12,)),
            pltpu.SemaphoreType.DMA((2,)),
        ],
        compiler_params=pltpu.CompilerParams(
            collective_id=0, has_side_effects=True, vmem_limit_bytes=56 << 20
        ),
    )(feat_in, coef_in, conv_first, bias_first[None], conv_second, bias_second[None])
    return out.reshape(scenes, planes, rows, regs * columns)


def solution(mesh):
    in_specs = (
        P(None, "rows", None),
        P(None, None, "rows", None),
        P(None, None, "depth", "rows"),
        P(None, None, "depth", "rows", None),
        P(),
        P(),
        P(),
        P(),
    )
    out_specs = P(None, "depth", "rows", None)
    step = functools.partial(body, mesh.shape["depth"], mesh.shape["rows"])
    return jax.shard_map(step, mesh=mesh, in_specs=in_specs, out_specs=out_specs, check_vma=False)
```

time: 117 us -> 64.3 us (0.55); the launches traced: 114 us -> 63.9 us
  Pallas kernels: 0 us -> 56.7 us
  waiting for transfers between devices: 31.8 us -> 0 us
  starting transfers between devices: 23.5 us -> 0 us
  local copies, waits for them, and re-layouts: 28.5 us -> 5.49 us
  matrix products: 16.8 us -> 0 us
  other arithmetic: 12 us -> 1.6 us
    pallas_call x0 -> x1, Pallas kernels: none -> 56.7 us  [body(): pl.pallas_call(functools.partial(kernel, dims), out_shape=jax.ShapeDtypeS...]
    ppermute x10 -> x0, waiting for transfers between devices: 31.8 us -> none  [the longest x5 19.6 us: extended(): lax.ppermute(lax.slice_in_dim(block, 0, width, axis=dim), axis, backward)]
    ppermute x10 -> x0, starting transfers between devices: 23.5 us -> none  [the longest x5 16.5 us: extended(): lax.ppermute(lax.slice_in_dim(block, block.shape[dim] - width, None, axis...]
    dot_general x54 -> x0, matrix products: 16.8 us -> none  [convolve(): jnp.einsum('bprcw,oc->bprow', piece, kernel[tap_depth, tap_row, tap_col],...]
    another operation x36 -> x0, local copies, waits for them, and re-layouts: 15.6 us -> none
    reduce_sum x18 -> x0, other arithmetic: 7.24 us -> none  [the longest x6 3.56 us: cost_plane(): jnp.sum(products, axis=(1, 4)) / (source_views * per_group * 1.0)]
    concatenate x9 -> x1, other arithmetic: 3.19 us -> 0.04 us  [body(): coef = jnp.concatenate([lower, upper], axis=1)]
    reshape x4 -> x2, local copies, waits for them, and re-layouts: 4.99 us -> 2.43 us  [the longest x1 2.29 us: body(): return out.reshape(scenes, planes, rows, regs * columns)]
  transfers between devices with their start and end apart: 10 -> 0, of which waited for: 8 -> 0; matrix products, arithmetic and copies ran while one was open for 2% -> 0% of each run, Pallas kernels for 0% -> 0%
where the time goes in v1:
time: 64.3 us; the launch traced here: 63.9 us
  Pallas kernels  56.7 us (88%)
  local copies, waits for them, and re-layouts  5.49 us (9%)
  other arithmetic  1.6 us (2%)
    pallas_call x1, Pallas kernels, body(): pl.pallas_call(functools.partial(kernel, dims), out_shape=jax.ShapeDtypeS...  56.7 us
    reshape x1, local copies, waits for them, and re-layouts, body(): return out.reshape(scenes, planes, rows, regs * columns)  2.29 us
    unnamed x7, local copies, waits for them, and re-layouts  1.46 us
    concatenate x3, local copies, waits for them, and re-layouts, body(): cube = jnp.concatenate([src_feat, ref_feat[:, None]], axis=1)  1.33 us

profile of v1, /device:TPU:0, one launch (start us, length us, event | category | flops | bytes accessed | tf_op | source)
XLA Modules:
  0.0 63.9 jit_solution(9404756597924207948)
XLA Ops:
  0.0 1.2 %concatenate.18 = bf16[2,4,2,8,4,160]{5,4,3,2,1,0:T(4,128)(2,1)S(1)} reshape(bf16[2,4,2,5120]{3,2,1,0:T(2,128)(2,1)} %param.9) | data formatting | bytes 327680 | tf_op jit(solution)/shard_map/concatenate | solution.py:285
  1.2 0.0 copy-start.1
  1.2 0.1 copy_dynamic-update-slice_fusion
  1.3 0.7 %copy-done.1 = bf16[2,2,5120]{2,1,0:T(2,128)(2,1)S(1)} copy-done((bf16[2,2,5120]{2,1,0:T(2,128)(2,1)S(1)}, bf16[2,2,5120]{2,1,0:T(2,128)(2,1)}, u32[]{:S(2)}) %copy-start.1) | copy-done | bytes 40984
  2.0 0.1 concatenate.19
  2.1 0.1 slice.15
  2.2 0.1 reshape.15
  2.3 0.1 slice_bitcast_fusion
  2.4 0.0 copy-start
  2.4 0.7 %maximum_bitcast_fusion.feat_in = bf16[5,2,2,40,128]{4,3,2,1,0:T(8,128)(2,1)} fusion(bf16[2,5,2,8,128]{4,3,2,0,1:T(8,128)(2,1)S(1)} %reshape.15, bf16[2,5,2,32,128]{4,3,2,0,1:T(8,128)(2,1)S(1)} %bitcast.16), kind=kLoop, calls=%fused_computation.1 | loop fusion | flops 409600 | bytes 409600 | tf_op jit(solution)/shard_map/transpose | solution.py:289
  3.1 0.0 copy-start.2
  3.1 0.7 %copy-done.2 = s32[2,4,6,1]{2,3,1,0:T(1,128)S(1)} copy-done((s32[2,4,6,1]{2,3,1,0:T(1,128)S(1)}, s32[2,4,6,1]{2,3,1,0:T(1,128)}, u32[]{:S(2)}) %copy-start.2) | copy-done | bytes 216
  3.8 0.1 copy.14
  4.0 0.0 copy-done
  4.0 0.1 broadcast_select_fusion.1
  4.1 0.7 %maximum_bitcast_fusion.1.coef_in = bf16[6,2,2,8,256]{4,3,2,1,0:T(8,128)(2,1)} fusion(bf16[2,8,6,2,32]{4,1,3,0,2:T(8,128)(2,1)S(1)} %pad_maximum_fusion, bf16[2,4,6,2,160]{4,1,3,0,2:T(4,128)(2,1)S(1)} %get-tuple-element.6, bf16[2,4,6,2,160]{4,1,3,0,2:T(4,128)(2,1)S(1)} %get-tuple-element.5), kind=kLoop, calls=%fused_computation.4 | loop fusion | flops 491520 | bytes 172032 | tf_op jit(solution)/shard_map/transpose | solution.py:296
  4.9 56.7 %shard_map.82 = bf16[2,6,2,32,160]{4,3,2,1,0:T(8,128)(2,1)} custom-call(bf16[5,2,2,40,128]{4,3,2,1,0:T(8,128)(2,1)} %maximum_bitcast_fusion.feat_in, bf16[6,2,2,8,256]{4,3,2,1,0:T(8,128)(2,1)} %maximum_bitcast_fusion.1.coef_in, bf16[3,3,3,32,40]{4,3,2,1,0:T(8,128)(2,1)} %k1_in.1, f32[1,32]{1,0:T(1,128)} %bitcast.18, bf16[3,3,3,32,32]{4,3,2,1,0:T(8,128)(2,1)} %k2_in.1, ...), custom_call_target="tpu_custom_call" | custom-call | tf_op jit(solution)/shard_map/pallas_call | solution.py:301
  61.6 2.3 %reshape.16 = bf16[2,6,2,5120]{3,2,1,0:T(2,128)(2,1)} reshape(bf16[2,6,2,32,160]{4,3,2,1,0:T(8,128)(2,1)} %shard_map.82) | data formatting | bytes 491520 | tf_op jit(solution)/shard_map/reshape | solution.py:324
  (4 shorter events, 0.1 us)
Async XLA Ops:
  1.2 0.8 %copy-start.1 = (bf16[2,2,5120]{2,1,0:T(2,128)(2,1)S(1)}, bf16[2,2,5120]{2,1,0:T(2,128)(2,1)}, u32[]{:S(2)}) copy-start(bf16[2,2,5120]{2,1,0:T(2,128)(2,1)} %param.8) | copy-start | bytes 122884
  2.4 1.5 %copy-start = (bf16[2,4,6,2,160]{4,3,2,1,0:T(2,128)(2,1)S(1)}, bf16[2,4,6,2,160]{4,3,2,1,0:T(2,128)(2,1)}, u32[]{:S(2)}) copy-start(bf16[2,4,6,2,160]{4,3,2,1,0:T(2,128)(2,1)} %param.11) | copy-start | bytes 92164
  3.1 0.7 %copy-start.2 = (s32[2,4,6,1]{2,3,1,0:T(1,128)S(1)}, s32[2,4,6,1]{2,3,1,0:T(1,128)}, u32[]{:S(2)}) copy-start(s32[2,4,6,1]{2,3,1,0:T(1,128)} %param.10) | copy-start | bytes 580

commit v2 on v1

--- a/solution.py
+++ b/solution.py
@@ -11,6 +11,11 @@
 LANES = 128
 NEAR = ((0, 1), (0, -1), (1, 0), (-1, 0), (1, 1), (1, -1), (-1, 1), (-1, -1))
 FAR = ((0, 2), (0, -2))
+
+
+def run(count, step, most=5):
+    unroll = max(k for k in range(1, most + 1) if count % k == 0)
+    lax.fori_loop(0, count, step, 0, unroll=unroll)
 
 
 def kernel(
@@ -21,10 +26,13 @@
     channels = groups + feats
     per_group = feats // groups
     packed = feat_in.shape[3]
+    half = scenes // 2
     wide = 2 * LANES
     tail = columns - LANES
     d = lax.axis_index("depth")
     q = lax.axis_index("rows")
+    side = lax.rem(d, 2)
+    mate = d + 1 - 2 * side
 
     def exists(dd, dq):
         return (d + dd >= 0) & (d + dd < depth_n) & (q + dq >= 0) & (q + dq < rows_n)
@@ -46,10 +54,20 @@
         slot = 2 - dq
         count = views + 1 if abs(dq) == 1 else views
         return pltpu.make_async_remote_copy(
-            src_ref=feat_in.at[pl.ds(0, count)],
-            dst_ref=feat.at[slot, pl.ds(0, count)],
+            src_ref=feat_in.at[pl.ds(side * half, half), pl.ds(0, count)],
+            dst_ref=feat.at[slot, pl.ds(side * half, half), pl.ds(0, count)],
             send_sem=send_sem.at[k], recv_sem=recv_sem.at[k],
             device_id=(d, q + dq), device_id_type=MESH,
+        )
+
+    def mate_copy(dq, k):
+        slot = 2 - dq
+        count = views + 1 if abs(dq) == 1 else views
+        part = feat.at[slot, pl.ds(side * half, half), pl.ds(0, count)]
+        return pltpu.make_async_remote_copy(
+            src_ref=part, dst_ref=part,
+            send_sem=send_sem.at[k], recv_sem=recv_sem.at[k],
+            device_id=(mate, q), device_id_type=MESH,
         )
 
     def coef_copy(dd, dq, k):
@@ -73,7 +91,9 @@
         ((dd, dq), coef_copy(dd, dq, 6 + i))
         for i, (dd, dq) in enumerate([m for m in NEAR if m[1] != 0])
     ]
-    every = depth_coef + near_feat + side_coef + far_feat
+    every = near_feat + depth_coef + side_coef + far_feat
+    near_mate = [((0, dq), mate_copy(dq, 12 + i)) for i, dq in enumerate((1, -1))]
+    far_mate = [((0, dq), mate_copy(dq, 14 + i)) for i, dq in enumerate((2, -2))]
 
     for slot, gone in ((0, q < 2), (1, q < 1), (3, q + 1 >= rows_n), (4, q + 2 >= rows_n)):
         @pl.when(gone)
@@ -95,6 +115,12 @@
             @pl.when(exists(-dd, -dq))
             def _():
                 copy.wait_recv()
+
+    def hand_on(pairs):
+        for (dd, dq), copy in pairs:
+            @pl.when(exists(-dd, -dq))
+            def _():
+                copy.start()
 
     def place(kernel_in, count, span, target, dest):
         for a in range(3):
@@ -141,12 +167,12 @@
     def volume_rows(block):
         for b in range(scenes):
             for m in range(rows):
-                ref = feat[block + 1, views, b, m].astype(jnp.float32)
+                ref = feat[block + 1, b, views, m].astype(jnp.float32)
                 prep[3 * views] = ref
                 for v in range(views):
-                    low = feat[block, v, b, m].astype(jnp.float32)
-                    mid = feat[block + 1, v, b, m].astype(jnp.float32)
-                    up = feat[block + 2, v, b, m].astype(jnp.float32)
+                    low = feat[block, b, v, m].astype(jnp.float32)
+                    mid = feat[block + 1, b, v, m].astype(jnp.float32)
+                    up = feat[block + 2, b, v, m].astype(jnp.float32)
                     prep[v] = mid - ref
                     prep[views + v] = low - mid
                     prep[2 * views + v] = up - mid
@@ -203,13 +229,17 @@
                     vol[b, p, row + rows] = jnp.concatenate(lines, axis=0).astype(jnp.bfloat16)
                     return carry
 
-                lax.fori_loop(0, planes + 4, plane, 0)
-
+                run(planes + 4, plane)
+
+    arrive(near_feat)
+    hand_on(near_mate)
     arrive(depth_coef)
-    arrive(near_feat)
+    arrive(near_mate)
     volume_rows(1)
+    arrive(far_feat)
+    hand_on(far_mate)
     arrive(side_coef)
-    arrive(far_feat)
+    arrive(far_mate)
     volume_rows(0)
     volume_rows(2)
 
@@ -224,7 +254,7 @@
                 work[p] = jnp.dot(w1[...], piece, preferred_element_type=jnp.float32)
                 return carry
 
-            lax.fori_loop(0, planes + 4, first, 0)
+            run(planes + 4, first)
 
             def hidden(p, carry):
                 summed = (
@@ -244,14 +274,14 @@
                     hid[b, p, base + j] = jnp.concatenate(lines, axis=0).astype(jnp.bfloat16)
                 return carry
 
-            lax.fori_loop(0, planes + 2, hidden, 0)
+            run(planes + 2, hidden)
 
         def second(p, carry):
             piece = hid[b, p].reshape((rows + 2) * LANES, wide)
             work[p] = jnp.dot(w2[...], piece, preferred_element_type=jnp.float32)
             return carry
 
-        lax.fori_loop(0, planes + 2, second, 0)
+        run(planes + 2, second)
 
         def finish(p, carry):
             summed = (
@@ -262,10 +292,15 @@
                 out_ref[b, p, j] = summed[j * regs : (j + 1) * regs, 0:columns].astype(jnp.bfloat16)
             return carry
 
-        lax.fori_loop(0, planes, finish, 0)
+        run(planes, finish)
 
     for (dd, dq), copy in every:
         @pl.when(exists(dd, dq))
+        def _():
+            copy.wait_send()
+
+    for (dd, dq), copy in near_mate + far_mate:
+        @pl.when(exists(-dd, -dq))
         def _():
             copy.wait_send()
 
@@ -286,7 +321,7 @@
     cube = cube.reshape(scenes, views + 1, rows, groups, per_group, columns)
     main = jnp.moveaxis(cube[..., :LANES], 4, 3).reshape(scenes, views + 1, rows, feats, LANES)
     ends = cube[..., LANES:].reshape(scenes, views + 1, rows, groups, per_group * tail)
-    feat_in = jnp.moveaxis(jnp.concatenate([main, ends], axis=3), 1, 0)
+    feat_in = jnp.concatenate([main, ends], axis=3)
 
     below = (block_index < lax.axis_index("rows"))[:, :, :, :, None]
     lower = jnp.where(below, blend, jnp.zeros_like(blend))
@@ -304,7 +339,7 @@
         in_specs=[pl.BlockSpec(memory_space=pltpu.VMEM)] * 6,
         out_specs=pl.BlockSpec(memory_space=pltpu.VMEM),
         scratch_shapes=[
-            pltpu.VMEM((5, views + 1, scenes, rows, packed, LANES), bf16),
+            pltpu.VMEM((5, scenes, views + 1, rows, packed, LANES), bf16),
             pltpu.VMEM((3, planes + 4, scenes, rows, 2 * views, wide), bf16),
             pltpu.VMEM((scenes, planes + 4, 3 * rows, LANES, wide), bf16),
             pltpu.VMEM((scenes, planes + 2, rows + 2, LANES, wide), bf16),
@@ -313,8 +348,8 @@
             pltpu.VMEM((3 * rows * regs, (rows + 2) * LANES), bf16),
             pltpu.VMEM((3 * views + 1, packed, LANES), f32),
             pltpu.VMEM((2, rows * regs, wide), f32),
-            pltpu.SemaphoreType.DMA((12,)),
-            pltpu.SemaphoreType.DMA((12,)),
+            pltpu.SemaphoreType.DMA((16,)),
+            pltpu.SemaphoreType.DMA((16,)),
             pltpu.SemaphoreType.DMA((2,)),
         ],
         compiler_params=pltpu.CompilerParams(

time: 64.3 us -> 37 us (0.58)
  Pallas kernels: 56.7 us -> 29.5 us
    pallas_call x1, Pallas kernels: 56.7 us -> 29.5 us  [body(): pl.pallas_call(functools.partial(kernel, dims), out_shape=jax.ShapeDtypeS...]
    concatenate x0 -> x2, other arithmetic: none -> 0.8 us  [the longest x1 0.7 us: body(): feat_in = jnp.concatenate([main, ends], axis=3)]
    unnamed x7 -> x4, local copies, waits for them, and re-layouts: 1.46 us -> 0.69 us
    concatenate x3 -> x2, local copies, waits for them, and re-layouts: 1.33 us -> 2.08 us  [body(): cube = jnp.concatenate([src_feat, ref_feat[:, None]], axis=1)]
where the time goes in v2:
time: 37 us; the launch traced here: 36.7 us
  Pallas kernels  29.5 us (80%)
  local copies, waits for them, and re-layouts  5.34 us (14%)
  other arithmetic  1.81 us (5%)
    pallas_call x1, Pallas kernels, body(): pl.pallas_call(functools.partial(kernel, dims), out_shape=jax.ShapeDtypeS...  29.5 us
    reshape x1, local copies, waits for them, and re-layouts, body(): return out.reshape(scenes, planes, rows, regs * columns)  2.29 us
    concatenate x2, local copies, waits for them, and re-layouts, body(): cube = jnp.concatenate([src_feat, ref_feat[:, None]], axis=1)  2.08 us
    transpose x1, other arithmetic, body(): coef_in = jnp.transpose(coef, (2, 0, 3, 1, 4))  0.74 us

profile of v2, /device:TPU:0, one launch (start us, length us, event | category | flops | bytes accessed | tf_op | source)
XLA Modules:
  0.0 36.7 jit_solution(725157945296595711)
XLA Ops:
  0.0 0.9 %concatenate.19 = bf16[2,1,2,8,4,160]{5,4,3,2,0,1:T(4,128)(2,1)S(1)} reshape(bf16[2,2,5120]{2,1,0:T(2,128)(2,1)} %param.8) | data formatting | bytes 81920 | tf_op jit(solution)/shard_map/concatenate | solution.py:320
  0.9 1.2 %concatenate.18 = bf16[2,4,2,8,4,160]{5,4,3,2,1,0:T(4,128)(2,1)S(1)} reshape(bf16[2,4,2,5120]{3,2,1,0:T(2,128)(2,1)} %param.9) | data formatting | bytes 327680 | tf_op jit(solution)/shard_map/concatenate | solution.py:320
  2.1 0.1 pad_maximum_fusion.1
  2.2 0.1 reshape.15
  2.3 0.1 fusion.1
  2.5 0.0 copy-start
  2.5 0.7 %pad_maximum_fusion.feat_in = bf16[2,5,2,40,128]{4,3,2,1,0:T(8,128)(2,1)} fusion(bf16[2,5,2,8,128]{4,3,2,1,0:T(8,128)(2,1)S(1)} %reshape.15, bf16[2,5,2,32,128]{4,3,2,1,0:T(8,128)(2,1)S(1)} %bitcast.13), kind=kLoop, calls=%fused_computation.2 | loop fusion | flops 409600 | bytes 409600 | tf_op jit(solution)/shard_map/concatenate | solution.py:324
  3.2 0.0 copy-start.1
  3.2 0.7 %copy-done.1 = s32[2,4,6,1]{2,3,1,0:T(1,128)S(1)} copy-done((s32[2,4,6,1]{2,3,1,0:T(1,128)S(1)}, s32[2,4,6,1]{2,3,1,0:T(1,128)}, u32[]{:S(2)}) %copy-start.1) | copy-done | bytes 216
  3.9 0.1 copy.14
  4.0 0.0 copy-done
  4.0 0.1 broadcast_select_fusion.1
  4.2 0.7 %maximum_bitcast_fusion.coef_in = bf16[6,2,2,8,256]{4,3,2,1,0:T(8,128)(2,1)} fusion(bf16[2,8,6,2,32]{4,1,3,0,2:T(8,128)(2,1)S(1)} %pad_maximum_fusion.2, bf16[2,4,6,2,160]{4,1,3,0,2:T(4,128)(2,1)S(1)} %get-tuple-element.6, bf16[2,4,6,2,160]{4,1,3,0,2:T(4,128)(2,1)S(1)} %get-tuple-element.5), kind=kLoop, calls=%fused_computation.7 | loop fusion | flops 491520 | bytes 172032 | tf_op jit(solution)/shard_map/transpose | solution.py:331
  4.9 29.5 %shard_map.82 = bf16[2,6,2,32,160]{4,3,2,1,0:T(8,128)(2,1)} custom-call(bf16[2,5,2,40,128]{4,3,2,1,0:T(8,128)(2,1)} %pad_maximum_fusion.feat_in, bf16[6,2,2,8,256]{4,3,2,1,0:T(8,128)(2,1)} %maximum_bitcast_fusion.coef_in, bf16[3,3,3,32,40]{4,3,2,1,0:T(8,128)(2,1)} %k1_in.1, f32[1,32]{1,0:T(1,128)} %bitcast.17, bf16[3,3,3,32,32]{4,3,2,1,0:T(8,128)(2,1)} %k2_in.1, ...), custom_call_target="tpu_custom_call" | custom-call | tf_op jit(solution)/shard_map/pallas_call | solution.py:336
  34.4 2.3 %reshape.16 = bf16[2,6,2,5120]{3,2,1,0:T(2,128)(2,1)} reshape(bf16[2,6,2,32,160]{4,3,2,1,0:T(8,128)(2,1)} %shard_map.82) | data formatting | bytes 491520 | tf_op jit(solution)/shard_map/reshape | solution.py:359
  (3 shorter events, 0.1 us)
Async XLA Ops:
  2.5 1.5 %copy-start = (bf16[2,4,6,2,160]{4,3,2,1,0:T(2,128)(2,1)S(1)}, bf16[2,4,6,2,160]{4,3,2,1,0:T(2,128)(2,1)}, u32[]{:S(2)}) copy-start(bf16[2,4,6,2,160]{4,3,2,1,0:T(2,128)(2,1)} %param.11) | copy-start | bytes 92164
  3.2 0.7 %copy-start.1 = (s32[2,4,6,1]{2,3,1,0:T(1,128)S(1)}, s32[2,4,6,1]{2,3,1,0:T(1,128)}, u32[]{:S(2)}) copy-start(s32[2,4,6,1]{2,3,1,0:T(1,128)} %param.10) | copy-start | bytes 580

commit v3 on v2

--- a/solution.py
+++ b/solution.py
@@ -91,7 +91,7 @@
         ((dd, dq), coef_copy(dd, dq, 6 + i))
         for i, (dd, dq) in enumerate([m for m in NEAR if m[1] != 0])
     ]
-    every = near_feat + depth_coef + side_coef + far_feat
+    every = near_feat + depth_coef + far_feat + side_coef
     near_mate = [((0, dq), mate_copy(dq, 12 + i)) for i, dq in enumerate((1, -1))]
     far_mate = [((0, dq), mate_copy(dq, 14 + i)) for i, dq in enumerate((2, -2))]
 
@@ -122,7 +122,7 @@
             def _():
                 copy.start()
 
-    def place(kernel_in, count, span, target, dest):
+    def place(kernel_in, count, span, target, dest, order=None):
         for a in range(3):
             for r in range(3):
                 line = jnp.zeros((regs, span), jnp.float32)
@@ -132,6 +132,9 @@
                     pick = jnp.where(dest(s, c) == k, 1.0, 0.0).astype(jnp.bfloat16)
                     line = line + jnp.dot(kernel_in[a, r, s], pick, preferred_element_type=jnp.float32)
                 line = line.astype(jnp.bfloat16)
+                if order is not None:
+                    line = jnp.dot(order, line, preferred_element_type=jnp.float32)
+                    line = line.astype(jnp.bfloat16)
                 for j in range(rows):
                     target[pl.ds((a * rows + j) * regs, regs), pl.ds((j + r) * span, span)] = line
 
@@ -143,12 +146,16 @@
     w1[...] = jnp.zeros(w1.shape, w1.dtype)
     w2[...] = jnp.zeros(w2.shape, w2.dtype)
     place(k1_in, channels, LANES, w1, first_dest)
-    place(k2_in, regs, LANES, w2, lambda s, c: s * regs + c)
-    eye = lax.broadcasted_iota(jnp.int32, (regs, regs), 0) == lax.broadcasted_iota(
-        jnp.int32, (regs, regs), 1
+    per_out = regs // groups
+    at_row = lax.broadcasted_iota(jnp.int32, (regs, regs), 0)
+    at_channel = lax.broadcasted_iota(jnp.int32, (regs, regs), 1)
+    order = at_channel == (at_row % groups) * per_out + at_row // groups
+    place(
+        k2_in, regs, LANES, w2, lambda s, c: s * regs + c,
+        jnp.where(order, 1.0, 0.0).astype(jnp.bfloat16),
     )
-    for i, b_in in enumerate((b1_in, b2_in)):
-        column = jnp.sum(jnp.where(eye, b_in[...], 0.0), axis=1, keepdims=True)
+    for i, (b_in, mask) in enumerate(((b1_in, at_row == at_channel), (b2_in, order))):
+        column = jnp.sum(jnp.where(mask, b_in[...], 0.0), axis=1, keepdims=True)
         bias[i] = jnp.broadcast_to(jnp.concatenate([column] * rows, axis=0), (rows * regs, wide))
 
     for copy in local:
@@ -238,28 +245,41 @@
     volume_rows(1)
     arrive(far_feat)
     hand_on(far_mate)
+
+    size = rows * regs
+
+    def products(own):
+        for b in range(scenes):
+            for pair in range(2):
+                start = rows if own else 2 * rows * pair
+                line = w1.at[:, pl.ds((start - pair * rows) * LANES, rows * LANES)]
+
+                def first(p, carry):
+                    piece = vol[b, p, pl.ds(start, rows)].reshape(rows * LANES, wide)
+                    value = jnp.dot(line[...], piece, preferred_element_type=jnp.float32)
+                    if not own:
+                        value = value + work[2 * b + pair, p]
+                    work[2 * b + pair, p] = value
+                    return carry
+
+                run(planes + 4, first)
+
+    products(True)
     arrive(side_coef)
     arrive(far_mate)
     volume_rows(0)
     volume_rows(2)
-
-    size = rows * regs
+    products(False)
     inside = lax.broadcasted_iota(jnp.int32, (regs, wide), 1) < columns
     for b in range(scenes):
         for pair in range(2):
             base = pair * rows
-
-            def first(p, carry):
-                piece = vol[b, p, pl.ds(base, rows + 2)].reshape((rows + 2) * LANES, wide)
-                work[p] = jnp.dot(w1[...], piece, preferred_element_type=jnp.float32)
-                return carry
-
-            run(planes + 4, first)
+            at_work = work.at[2 * b + pair]
 
             def hidden(p, carry):
                 summed = (
-                    work[p, 0:size] + work[p + 1, size : 2 * size]
-                    + work[p + 2, 2 * size : 3 * size] + bias[0]
+                    at_work[p, 0:size] + at_work[p + 1, size : 2 * size]
+                    + at_work[p + 2, 2 * size : 3 * size] + bias[0]
                 )
                 summed = jnp.maximum(summed, 0.0)
                 at = d * planes + p - 1
@@ -278,18 +298,21 @@
 
         def second(p, carry):
             piece = hid[b, p].reshape((rows + 2) * LANES, wide)
-            work[p] = jnp.dot(w2[...], piece, preferred_element_type=jnp.float32)
+            work[0, p] = jnp.dot(w2[...], piece, preferred_element_type=jnp.float32)
             return carry
 
         run(planes + 2, second)
 
         def finish(p, carry):
             summed = (
-                work[p, 0:size] + work[p + 1, size : 2 * size]
-                + work[p + 2, 2 * size : 3 * size] + bias[1]
+                work[0, p, 0:size] + work[0, p + 1, size : 2 * size]
+                + work[0, p + 2, 2 * size : 3 * size] + bias[1]
             )
             for j in range(rows):
-                out_ref[b, p, j] = summed[j * regs : (j + 1) * regs, 0:columns].astype(jnp.bfloat16)
+                for t in range(per_out):
+                    first_row = j * regs + t * groups
+                    part = summed[first_row : first_row + groups, 0:columns]
+                    out_ref[b, p, j, :, pl.ds(t * columns, columns)] = part.astype(jnp.bfloat16)
             return carry
 
         run(planes, finish)
@@ -335,7 +358,7 @@
     bf16, f32 = jnp.bfloat16, jnp.float32
     out = pl.pallas_call(
         functools.partial(kernel, dims),
-        out_shape=jax.ShapeDtypeStruct((scenes, planes, rows, regs, columns), bf16),
+        out_shape=jax.ShapeDtypeStruct((scenes, planes, rows, groups, regs // groups * columns), bf16),
         in_specs=[pl.BlockSpec(memory_space=pltpu.VMEM)] * 6,
         out_specs=pl.BlockSpec(memory_space=pltpu.VMEM),
         scratch_shapes=[
@@ -343,7 +366,7 @@
             pltpu.VMEM((3, planes + 4, scenes, rows, 2 * views, wide), bf16),
             pltpu.VMEM((scenes, planes + 4, 3 * rows, LANES, wide), bf16),
             pltpu.VMEM((scenes, planes + 2, rows + 2, LANES, wide), bf16),
-            pltpu.VMEM((planes + 4, 3 * rows * regs, wide), f32),
+            pltpu.VMEM((2 * scenes, planes + 4, 3 * rows * regs, wide), f32),
             pltpu.VMEM((3 * rows * regs, (rows + 2) * LANES), bf16),
             pltpu.VMEM((3 * rows * regs, (rows + 2) * LANES), bf16),
             pltpu.VMEM((3 * views + 1, packed, LANES), f32),

time: 37 us -> 34.1 us (0.922)
  Pallas kernels: 29.5 us -> 27.1 us
  local copies, waits for them, and re-layouts: 5.34 us -> 4.75 us
    pallas_call x1, Pallas kernels: 29.5 us -> 27.1 us  [body(): pl.pallas_call(functools.partial(kernel, dims), out_shape=jax.ShapeDtypeS...]
    reshape x1, local copies, waits for them, and re-layouts: 2.29 us -> 1.7 us  [body(): return out.reshape(scenes, planes, rows, regs * columns)]
where the time goes in v3:
time: 34.1 us; the launch traced here: 33.7 us
  Pallas kernels  27.1 us (79%)
  local copies, waits for them, and re-layouts  4.75 us (14%)
  other arithmetic  1.83 us (5%)
    pallas_call x1, Pallas kernels, body(): pl.pallas_call(functools.partial(kernel, dims), out_shape=jax.ShapeDtypeS...  27.1 us
    concatenate x2, local copies, waits for them, and re-layouts, body(): cube = jnp.concatenate([src_feat, ref_feat[:, None]], axis=1)  2.08 us
    reshape x1, local copies, waits for them, and re-layouts, body(): return out.reshape(scenes, planes, rows, regs * columns)  1.7 us
    transpose x1, other arithmetic, body(): coef_in = jnp.transpose(coef, (2, 0, 3, 1, 4))  0.76 us
    concatenate x1, other arithmetic, body(): feat_in = jnp.concatenate([main, ends], axis=3)  0.7 us
    unnamed x4, local copies, waits for them, and re-layouts  0.69 us

profile of v3, /device:TPU:0, one launch (start us, length us, event | category | flops | bytes accessed | tf_op | source)
XLA Modules:
  0.0 33.7 jit_solution(5449488142541231119)
XLA Ops:
  0.0 0.9 %concatenate.19 = bf16[2,1,2,8,4,160]{5,4,3,2,0,1:T(4,128)(2,1)S(1)} reshape(bf16[2,2,5120]{2,1,0:T(2,128)(2,1)} %param.8) | data formatting | bytes 81920 | tf_op jit(solution)/shard_map/concatenate | solution.py:343
  0.9 1.2 %concatenate.18 = bf16[2,4,2,8,4,160]{5,4,3,2,1,0:T(4,128)(2,1)S(1)} reshape(bf16[2,4,2,5120]{3,2,1,0:T(2,128)(2,1)} %param.9) | data formatting | bytes 327680 | tf_op jit(solution)/shard_map/concatenate | solution.py:343
  2.1 0.1 pad_maximum_fusion.1
  2.2 0.1 reshape.15
  2.3 0.1 fusion.1
  2.5 0.0 copy-start
  2.5 0.7 %pad_maximum_fusion.feat_in = bf16[2,5,2,40,128]{4,3,2,1,0:T(8,128)(2,1)} fusion(bf16[2,5,2,8,128]{4,3,2,1,0:T(8,128)(2,1)S(1)} %reshape.15, bf16[2,5,2,32,128]{4,3,2,1,0:T(8,128)(2,1)S(1)} %bitcast.13), kind=kLoop, calls=%fused_computation.2 | loop fusion | flops 409600 | bytes 409600 | tf_op jit(solution)/shard_map/concatenate | solution.py:347
  3.2 0.0 copy-start.1
  3.2 0.7 %copy-done.1 = s32[2,4,6,1]{2,3,1,0:T(1,128)S(1)} copy-done((s32[2,4,6,1]{2,3,1,0:T(1,128)S(1)}, s32[2,4,6,1]{2,3,1,0:T(1,128)}, u32[]{:S(2)}) %copy-start.1) | copy-done | bytes 216
  3.9 0.1 copy.14
  4.0 0.0 copy-done
  4.0 0.1 broadcast_select_fusion.1
  4.2 0.8 %maximum_bitcast_fusion.coef_in = bf16[6,2,2,8,256]{4,3,2,1,0:T(8,128)(2,1)} fusion(bf16[2,8,6,2,32]{4,1,3,0,2:T(8,128)(2,1)S(1)} %pad_maximum_fusion.2, bf16[2,4,6,2,160]{4,1,3,0,2:T(4,128)(2,1)S(1)} %get-tuple-element.6, bf16[2,4,6,2,160]{4,1,3,0,2:T(4,128)(2,1)S(1)} %get-tuple-element.5), kind=kLoop, calls=%fused_computation.7 | loop fusion | flops 491520 | bytes 172032 | tf_op jit(solution)/shard_map/transpose | solution.py:354
  5.0 27.1 %shard_map.82 = bf16[2,6,2,8,640]{4,3,2,1,0:T(8,128)(2,1)} custom-call(bf16[2,5,2,40,128]{4,3,2,1,0:T(8,128)(2,1)} %pad_maximum_fusion.feat_in, bf16[6,2,2,8,256]{4,3,2,1,0:T(8,128)(2,1)} %maximum_bitcast_fusion.coef_in, bf16[3,3,3,32,40]{4,3,2,1,0:T(8,128)(2,1)} %k1_in.1, f32[1,32]{1,0:T(1,128)} %bitcast.17, bf16[3,3,3,32,32]{4,3,2,1,0:T(8,128)(2,1)} %k2_in.1, ...), custom_call_target="tpu_custom_call" | custom-call | tf_op jit(solution)/shard_map/pallas_call | solution.py:359
  32.0 1.7 %reshape.16 = bf16[2,6,2,5120]{3,2,1,0:T(2,128)(2,1)} reshape(bf16[2,6,2,8,640]{4,3,2,1,0:T(8,128)(2,1)} %shard_map.82) | data formatting | bytes 491520 | tf_op jit(solution)/shard_map/reshape | solution.py:382
  (3 shorter events, 0.1 us)
Async XLA Ops:
  2.5 1.5 %copy-start = (bf16[2,4,6,2,160]{4,3,2,1,0:T(2,128)(2,1)S(1)}, bf16[2,4,6,2,160]{4,3,2,1,0:T(2,128)(2,1)}, u32[]{:S(2)}) copy-start(bf16[2,4,6,2,160]{4,3,2,1,0:T(2,128)(2,1)} %param.11) | copy-start | bytes 92164
  3.2 0.7 %copy-start.1 = (s32[2,4,6,1]{2,3,1,0:T(1,128)S(1)}, s32[2,4,6,1]{2,3,1,0:T(1,128)}, u32[]{:S(2)}) copy-start(s32[2,4,6,1]{2,3,1,0:T(1,128)} %param.10) | copy-start | bytes 580

commit v4 on v3

--- a/solution.py
+++ b/solution.py
@@ -13,14 +13,14 @@
 FAR = ((0, 2), (0, -2))
 
 
-def run(count, step, most=5):
+def run(count, step, most=8):
     unroll = max(k for k in range(1, most + 1) if count % k == 0)
     lax.fori_loop(0, count, step, 0, unroll=unroll)
 
 
 def kernel(
-    dims, feat_in, coef_in, k1_in, b1_in, k2_in, b2_in, out_ref,
-    feat, coef, vol, hid, work, w1, w2, prep, bias, send_sem, recv_sem, local_sem,
+    dims, feat_in, coef_in, k1_hbm, b1_in, k2_hbm, b2_in, out_ref,
+    k1_in, k2_in, feat, coef, vol, hid, work, w1, w2, prep, bias, send_sem, recv_sem, local_sem,
 ):
     scenes, views, rows, planes, feats, groups, columns, regs, depth_n, rows_n = dims
     channels = groups + feats
@@ -43,11 +43,15 @@
         def _():
             pl.semaphore_signal(barrier, inc=1, device_id=(d + dd, q + dq), device_id_type=MESH)
 
+    taps = [
+        pltpu.make_async_copy(k1_hbm, k1_in, local_sem.at[2]),
+        pltpu.make_async_copy(k2_hbm, k2_in, local_sem.at[3]),
+    ]
     local = [
         pltpu.make_async_copy(feat_in, feat.at[2], local_sem.at[0]),
         pltpu.make_async_copy(coef_in, coef.at[1, pl.ds(2, planes)], local_sem.at[1]),
     ]
-    for copy in local:
+    for copy in taps + local:
         copy.start()
 
     def feat_copy(dq, k):
@@ -145,6 +149,8 @@
 
     w1[...] = jnp.zeros(w1.shape, w1.dtype)
     w2[...] = jnp.zeros(w2.shape, w2.dtype)
+    for copy in taps:
+        copy.wait()
     place(k1_in, channels, LANES, w1, first_dest)
     per_out = regs // groups
     at_row = lax.broadcasted_iota(jnp.int32, (regs, regs), 0)
@@ -359,9 +365,18 @@
     out = pl.pallas_call(
         functools.partial(kernel, dims),
         out_shape=jax.ShapeDtypeStruct((scenes, planes, rows, groups, regs // groups * columns), bf16),
-        in_specs=[pl.BlockSpec(memory_space=pltpu.VMEM)] * 6,
+        in_specs=[
+            pl.BlockSpec(memory_space=pl.ANY),
+            pl.BlockSpec(memory_space=pl.ANY),
+            pl.BlockSpec(memory_space=pl.ANY),
+            pl.BlockSpec(memory_space=pltpu.VMEM),
+            pl.BlockSpec(memory_space=pl.ANY),
+            pl.BlockSpec(memory_space=pltpu.VMEM),
+        ],
         out_specs=pl.BlockSpec(memory_space=pltpu.VMEM),
         scratch_shapes=[
+            pltpu.VMEM(conv_first.shape, bf16),
+            pltpu.VMEM(conv_second.shape, bf16),
             pltpu.VMEM((5, scenes, views + 1, rows, packed, LANES), bf16),
             pltpu.VMEM((3, planes + 4, scenes, rows, 2 * views, wide), bf16),
             pltpu.VMEM((scenes, planes + 4, 3 * rows, LANES, wide), bf16),
@@ -373,7 +388,7 @@
             pltpu.VMEM((2, rows * regs, wide), f32),
             pltpu.SemaphoreType.DMA((16,)),
             pltpu.SemaphoreType.DMA((16,)),
-            pltpu.SemaphoreType.DMA((2,)),
+            pltpu.SemaphoreType.DMA((4,)),
         ],
         compiler_params=pltpu.CompilerParams(
             collective_id=0, has_side_effects=True, vmem_limit_bytes=56 << 20

time: 34.1 us -> 32.1 us (0.941)
  Pallas kernels: 27.1 us -> 25.1 us
    pallas_call x1, Pallas kernels: 27.1 us -> 25.1 us  [body(): pl.pallas_call(functools.partial(kernel, dims), out_shape=jax.ShapeDtypeS...]
where the time goes in v4:
time: 32.1 us; the launch traced here: 31.7 us
  Pallas kernels  25.1 us (78%)
  local copies, waits for them, and re-layouts  4.75 us (15%)
  other arithmetic  1.83 us (6%)
    pallas_call x1, Pallas kernels, body(): pl.pallas_call(functools.partial(kernel, dims), out_shape=jax.ShapeDtypeS...  25.1 us
    concatenate x2, local copies, waits for them, and re-layouts, body(): cube = jnp.concatenate([src_feat, ref_feat[:, None]], axis=1)  2.08 us
    reshape x1, local copies, waits for them, and re-layouts, body(): return out.reshape(scenes, planes, rows, regs * columns)  1.7 us
    transpose x1, other arithmetic, body(): coef_in = jnp.transpose(coef, (2, 0, 3, 1, 4))  0.76 us
    concatenate x1, other arithmetic, body(): feat_in = jnp.concatenate([main, ends], axis=3)  0.7 us
    unnamed x4, local copies, waits for them, and re-layouts  0.69 us

profile of v4, /device:TPU:0, one launch (start us, length us, event | category | flops | bytes accessed | tf_op | source)
XLA Modules:
  0.0 31.7 jit_solution(5695937756832248014)
XLA Ops:
  0.0 0.9 %concatenate.19 = bf16[2,1,2,8,4,160]{5,4,3,2,0,1:T(4,128)(2,1)S(1)} reshape(bf16[2,2,5120]{2,1,0:T(2,128)(2,1)} %param.8) | data formatting | bytes 81920 | tf_op jit(solution)/shard_map/concatenate | solution.py:349
  0.9 1.2 %concatenate.18 = bf16[2,4,2,8,4,160]{5,4,3,2,1,0:T(4,128)(2,1)S(1)} reshape(bf16[2,4,2,5120]{3,2,1,0:T(2,128)(2,1)} %param.9) | data formatting | bytes 327680 | tf_op jit(solution)/shard_map/concatenate | solution.py:349
  2.1 0.1 pad_maximum_fusion.1
  2.2 0.1 reshape.15
  2.3 0.1 fusion.1
  2.5 0.0 copy-start
  2.5 0.7 %pad_maximum_fusion.feat_in = bf16[2,5,2,40,128]{4,3,2,1,0:T(8,128)(2,1)} fusion(bf16[2,5,2,8,128]{4,3,2,1,0:T(8,128)(2,1)S(1)} %reshape.15, bf16[2,5,2,32,128]{4,3,2,1,0:T(8,128)(2,1)S(1)} %bitcast.13), kind=kLoop, calls=%fused_computation.2 | loop fusion | flops 409600 | bytes 409600 | tf_op jit(solution)/shard_map/concatenate | solution.py:353
  3.2 0.0 copy-start.1
  3.2 0.7 %copy-done.1 = s32[2,4,6,1]{2,3,1,0:T(1,128)S(1)} copy-done((s32[2,4,6,1]{2,3,1,0:T(1,128)S(1)}, s32[2,4,6,1]{2,3,1,0:T(1,128)}, u32[]{:S(2)}) %copy-start.1) | copy-done | bytes 216
  3.9 0.1 copy.14
  4.0 0.0 copy-done
  4.0 0.1 broadcast_select_fusion.1
  4.2 0.8 %maximum_bitcast_fusion.coef_in = bf16[6,2,2,8,256]{4,3,2,1,0:T(8,128)(2,1)} fusion(bf16[2,8,6,2,32]{4,1,3,0,2:T(8,128)(2,1)S(1)} %pad_maximum_fusion.2, bf16[2,4,6,2,160]{4,1,3,0,2:T(4,128)(2,1)S(1)} %get-tuple-element.6, bf16[2,4,6,2,160]{4,1,3,0,2:T(4,128)(2,1)S(1)} %get-tuple-element.5), kind=kLoop, calls=%fused_computation.7 | loop fusion | flops 491520 | bytes 172032 | tf_op jit(solution)/shard_map/transpose | solution.py:360
  5.0 25.1 %shard_map.82 = bf16[2,6,2,8,640]{4,3,2,1,0:T(8,128)(2,1)} custom-call(bf16[2,5,2,40,128]{4,3,2,1,0:T(8,128)(2,1)} %pad_maximum_fusion.feat_in, bf16[6,2,2,8,256]{4,3,2,1,0:T(8,128)(2,1)} %maximum_bitcast_fusion.coef_in, bf16[3,3,3,32,40]{4,3,2,1,0:T(8,128)(2,1)} %k1_hbm.1, f32[1,32]{1,0:T(1,128)} %bitcast.17, bf16[3,3,3,32,32]{4,3,2,1,0:T(8,128)(2,1)} %k2_hbm.1, ...), custom_call_target="tpu_custom_call" | custom-call | tf_op jit(solution)/shard_map/pallas_call | solution.py:365
  30.0 1.7 %reshape.16 = bf16[2,6,2,5120]{3,2,1,0:T(2,128)(2,1)} reshape(bf16[2,6,2,8,640]{4,3,2,1,0:T(8,128)(2,1)} %shard_map.82) | data formatting | bytes 491520 | tf_op jit(solution)/shard_map/reshape | solution.py:397
  (3 shorter events, 0.1 us)
Async XLA Ops:
  2.5 1.5 %copy-start = (bf16[2,4,6,2,160]{4,3,2,1,0:T(2,128)(2,1)S(1)}, bf16[2,4,6,2,160]{4,3,2,1,0:T(2,128)(2,1)}, u32[]{:S(2)}) copy-start(bf16[2,4,6,2,160]{4,3,2,1,0:T(2,128)(2,1)} %param.11) | copy-start | bytes 92164
  3.2 0.7 %copy-start.1 = (s32[2,4,6,1]{2,3,1,0:T(1,128)S(1)}, s32[2,4,6,1]{2,3,1,0:T(1,128)}, u32[]{:S(2)}) copy-start(s32[2,4,6,1]{2,3,1,0:T(1,128)} %param.10) | copy-start | bytes 580
